TPU v7x, 32 devices: a whole 2x2x4 slice. The times are simulated.
32 devices in a mesh: tm: 8 (over z, x), rows: 4 (over y, core).
Axes of the slice: x: 2, y: 2, z: 4, core: 2. Of those that a mesh axis runs over, the one named last changes fastest.
Arguments:
- sensed_flows_levels: float32 [32, 512], P('tm'), may hold values from -6 to 6
- reading_mask: int32 [32, 512], P('tm'), may hold values 0 or 1
- inventory_propagator: float32 [1024, 1024], replicated, may hold values from -1 to 1
- observation_matrix: float32 [512, 1024], replicated, may hold values from -0.1875 to 0.1875
- measurement_weight: float32 [512], replicated, may hold values from 0.05 to 0.3
- diagonal_blend_factor: float32 [32, 1024], P('tm', 'rows'), may hold values from 0 to 1
- prior_inventory_mean: float32 [1024], replicated, may hold values from -6 to 6
Outputs:
- updated_inventory_means: float32 [32, 1024], P('tm', 'rows')
- reconciled_inventories: float32 [32, 1024], P('tm', 'rows')
All inputs are finite; a program needn't handle non-finite values. No bound on the sum of `reading_mask` on one device may be relied on, other than what follows from the above.
Results may differ from a plain program's by a relative error of at most 0.0003.
Values sent between devices are 32-bit elements; how exact they have to be, the bound alone decides.
A program may use at most 64 MiB of HBM per device.

v0:
```python
import functools

import jax
import jax.numpy as jnp
from jax import lax
from jax.experimental import pallas as pl
from jax.experimental.pallas import tpu as pltpu
from jax.sharding import PartitionSpec as P

MESH = pl.DeviceIdType.MESH
CHUNK = 128
SHARES = (2, 0, 2)


def turned(rows, by):
    return pltpu.roll(rows, by, 0)


def split_rows(rows):
    high = rows.astype(jnp.bfloat16).astype(jnp.float32)
    even = lax.broadcasted_iota(jnp.int32, rows.shape, 0) % 2 == 0
    return jnp.where(even, high, rows - high).astype(jnp.bfloat16)


def apply(rows, plain, high, low):
    outputs, depth = plain.shape
    if high is not None:
        left = split_rows(rows)
        upper = jnp.dot(left, high[...], preferred_element_type=jnp.float32)
        lower = jnp.dot(left, low[...], preferred_element_type=jnp.float32)
    parts = []
    for first in range(0, outputs, CHUNK):
        sums = None
        for at in range(0, depth, CHUNK):
            block = plain[first : first + CHUNK, at : at + CHUNK].reshape(CHUNK // 8, 8, CHUNK)
            term = block * rows[None, :, at : at + CHUNK]
            sums = term if sums is None else sums + term
        part = jnp.sum(sums.reshape(CHUNK, CHUNK).T.reshape(CHUNK // 8, 8, CHUNK), axis=0)
        for by in (4, 2, 1):
            part += turned(part, by)
        parts.append(part)
    if high is not None:
        total = upper + lower
        parts.append(total + turned(total, 1))
    return jnp.concatenate(parts, axis=1)


def matrix_part(size, eighths):
    return size * eighths // 8 // CHUNK * CHUNK


def halves(value):
    high = value.astype(jnp.bfloat16)
    return high, (value - high.astype(jnp.float32)).astype(jnp.bfloat16)


def kernel(
    z_ref, m_ref, f_hbm, h_hbm, mw_ref, g_ref, x0_ref,
    out_ref,
    z_all, m_all, g_all, f_in, h_in, ft_hi, ft_lo, ht_hi, ht_lo, h_hi, h_lo, ht_in, xs, ps,
    send_sem, recv_sem, load_sem,
):
    me = lax.axis_index("tm")
    count = lax.axis_size("tm")
    steps = z_ref.shape[0]
    width = f_hbm.shape[0]
    measures = h_hbm.shape[0]
    own = g_ref.shape[1]
    f_chunks, h_chunks = width // CHUNK, measures // CHUNK

    def load(c):
        if c < h_chunks:
            rows = pl.ds(c * CHUNK, CHUNK)
            return pltpu.make_async_copy(h_hbm.at[rows], h_in.at[rows], load_sem.at[c])
        rows = pl.ds((c - h_chunks) * CHUNK, CHUNK)
        return pltpu.make_async_copy(f_hbm.at[rows], f_in.at[rows], load_sem.at[c])

    for c in range(f_chunks + h_chunks):
        load(c).start()

    barrier = pltpu.get_barrier_semaphore()

    @pl.loop(1, count)
    def _(d):
        peer = lax.rem(me + d, count)
        pl.semaphore_signal(barrier, inc=1, device_id={"tm": peer}, device_id_type=MESH)

    pl.semaphore_wait(barrier, count - 1)

    pairs = ((z_ref, z_all), (m_ref, m_all), (g_ref, g_all))

    def send(i, d):
        peer = lax.rem(me + d, count)
        return pltpu.make_async_remote_copy(
            src_ref=pairs[i][0], dst_ref=pairs[i][1].at[me],
            send_sem=send_sem.at[i, d], recv_sem=recv_sem.at[i, me],
            device_id={"tm": peer}, device_id_type=MESH,
        )

    def arrival(i, t):
        return pltpu.make_async_remote_copy(
            src_ref=pairs[i][0], dst_ref=pairs[i][1].at[t],
            send_sem=send_sem.at[i, 0], recv_sem=recv_sem.at[i, t],
            device_id={"tm": lax.rem(me + 1, count)}, device_id_type=MESH,
        )

    @pl.loop(1, count)
    def _(d):
        for i in range(3):
            send(i, d).start()

    z_all[me] = z_ref[...]
    m_all[me] = m_ref[...]
    g_all[me] = g_ref[...]

    f_part, q_part, u_part = shares(width, measures)
    f_plain, q_plain, u_plain = width - f_part, measures - q_part, width - u_part
    for c in range(h_chunks):
        load(c).wait()
        rows = pl.ds(c * CHUNK, CHUNK)
        ht_in[:, rows] = h_in[rows, :u_plain].T
        if u_part:
            h_hi[rows, :], h_lo[rows, :] = halves(h_in[rows, u_plain:])
        if c * CHUNK >= q_plain:
            to = pl.ds(c * CHUNK - q_plain, CHUNK)
            ht_hi[:, to], ht_lo[:, to] = halves(h_in[rows, :].T)
    for c in range(f_chunks):
        load(h_chunks + c).wait()
        if c * CHUNK >= f_plain:
            to = pl.ds(c * CHUNK - f_plain, CHUNK)
            ft_hi[:, to], ft_lo[:, to] = halves(f_in[pl.ds(c * CHUNK, CHUNK), :].T)

    nothing = (None, None)
    propagate = (f_in.at[:f_plain], *((ft_hi, ft_lo) if f_part else nothing))
    observe = (h_in.at[:q_plain], *((ht_hi, ht_lo) if q_part else nothing))
    spread = (ht_in, *((h_hi, h_lo) if u_part else nothing))

    def block_of_steps(t, predicted):
        @pl.when(t != me)
        def _():
            arrival(0, t).wait_recv()
            arrival(1, t).wait_recv()

        weights = m_all[t].astype(jnp.float32) * mw_ref[...]
        readings = z_all[t]
        alike = functools.partial(jnp.broadcast_to, shape=(8, measures))
        for k in range(steps):
            seen = apply(predicted, *observe)
            change = alike(weights[k : k + 1]) * (alike(readings[k : k + 1]) - seen)
            state = predicted + apply(change, *spread)
            predicted = apply(state, *propagate)
            xs[t, k : k + 1, :] = state[:1]
            ps[t, k : k + 1, :] = predicted[:1]
        return predicted

    lax.fori_loop(0, count, block_of_steps, apply(jnp.broadcast_to(x0_ref[...], (8, width)), *propagate))

    columns = pl.ds(pl.multiple_of(lax.axis_index("rows") * own, own), own)

    @pl.loop(0, count)
    def _(t):
        @pl.when(t != me)
        def _():
            arrival(2, t).wait_recv()

    def smooth(lap, later):
        t = count - 1 - lap
        means = xs[t, :, columns]
        priors = ps[t, :, columns]
        gains = g_all[t]
        rows = []
        for k in reversed(range(steps)):
            later = means[k : k + 1] + gains[k : k + 1] * (later - priors[k : k + 1])
            rows.insert(0, later)

        @pl.when(t == me)
        def _():
            out_ref[0] = means
            for k in range(steps):
                out_ref[1, k : k + 1, :] = rows[k]

        return later

    lax.fori_loop(0, count - me, smooth, ps[count - 1, steps - 1 : steps, columns])

    @pl.loop(1, count)
    def _(d):
        for i in range(3):
            send(i, d).wait_send()


def shares(width, measures):
    return tuple(map(matrix_part, (width, measures, width), SHARES))


def parted(both_ref, mean_ref, rec_ref):
    mean_ref[...] = both_ref[0]
    rec_ref[...] = both_ref[1]


def body(z, mask, f, h, mw, gain, x0):
    count = lax.axis_size("tm")
    steps, measures = z.shape
    width = f.shape[0]
    own = gain.shape[1]
    vmem = pl.BlockSpec(memory_space=pltpu.VMEM)
    hbm = pl.BlockSpec(memory_space=pl.ANY)
    out = jax.ShapeDtypeStruct((steps, own), jnp.float32)
    half = jnp.bfloat16
    f_part, q_part, u_part = shares(width, measures)
    both = pl.pallas_call(
        kernel,
        out_shape=jax.ShapeDtypeStruct((2, steps, own), jnp.float32),
        in_specs=[vmem, vmem, hbm, hbm, vmem, vmem, vmem],
        out_specs=vmem,
        scratch_shapes=[
            pltpu.VMEM((count, steps, measures), jnp.float32),
            pltpu.VMEM((count, steps, measures), jnp.int32),
            pltpu.VMEM((count, steps, own), jnp.float32),
            pltpu.VMEM((width, width), jnp.float32),
            pltpu.VMEM((measures, width), jnp.float32),
            pltpu.VMEM((width, max(f_part, CHUNK)), half),
            pltpu.VMEM((width, max(f_part, CHUNK)), half),
            pltpu.VMEM((width, max(q_part, CHUNK)), half),
            pltpu.VMEM((width, max(q_part, CHUNK)), half),
            pltpu.VMEM((measures, max(u_part, CHUNK)), half),
            pltpu.VMEM((measures, max(u_part, CHUNK)), half),
            pltpu.VMEM((width - u_part, measures), jnp.float32),
            pltpu.VMEM((count, steps, width), jnp.float32),
            pltpu.VMEM((count, steps, width), jnp.float32),
            pltpu.SemaphoreType.DMA((3, count)),
            pltpu.SemaphoreType.DMA((3, count)),
            pltpu.SemaphoreType.DMA(((width + measures) // CHUNK,)),
        ],
        compiler_params=pltpu.CompilerParams(
            collective_id=0, has_side_effects=True, vmem_limit_bytes=60 * 2**20
        ),
    )(z, mask, f, h, mw.reshape(1, -1), gain, x0.reshape(1, -1))
    return pl.pallas_call(
        parted, out_shape=(out, out), in_specs=[vmem], out_specs=(vmem, vmem)
    )(both)


def solution(mesh):
    placed = (P("tm", None), P("tm", None), P(), P(), P(), P("tm", "rows"), P())
    return jax.shard_map(
        body,
        mesh=mesh,
        in_specs=placed,
        out_specs=(P("tm", "rows"), P("tm", "rows")),
        check_vma=False,
    )
```

profile of v0, /device:TPU:0, one launch (start us, length us, event | category | flops | bytes accessed | tf_op | source)
XLA Modules:
  0.0 32.1 jit_solution(9291044893876797668)
XLA Ops:
  0.6 30.2 %shard_map.86.both_ref = f32[2,4,256]{2,1,0:T(4,128)} custom-call(f32[4,512]{1,0:T(4,128)} %z_ref.1, s32[4,512]{1,0:T(4,128)} %m_ref.1, f32[1024,1024]{1,0:T(8,128)} %f_hbm.1, f32[512,1024]{1,0:T(8,128)} %h_hbm.1, f32[1,512]{1,0:T(1,128)} %bitcast.3, f32[4,256]{1,0:T(4,128)} %g_ref.1, f32[1,1024]{1,0:T(1,128)} %bitcast.2), custom_call_target="tpu_custom_call" | custom-call | tf_op jit(solution)/shard_map/pallas_call | solution.py:211
  30.8 1.3 %shard_map.87 = (f32[4,256]{1,0:T(4,128)}, f32[4,256]{1,0:T(4,128)}) custom-call(f32[2,4,256]{2,1,0:T(4,128)} %shard_map.86.both_ref), custom_call_target="tpu_custom_call" | custom-call | tf_op jit(solution)/shard_map/pallas_call | solution.py:239
where the time goes:
time: 32.6 us; the launch traced here: 32.1 us
  Pallas kernels  31.5 us (97%)
  between operations  0.64 us (2%)
    pallas_call x1, Pallas kernels, body(): pl.pallas_call(kernel, out_shape=jax.ShapeDtypeStruct((2, steps, own), jn...  30.2 us
    pallas_call x1, Pallas kernels, body(): pl.pallas_call(parted, out_shape=(out, out), in_specs=[vmem], out_specs=(...  1.3 us

commit v1 on v0

--- a/solution.py
+++ b/solution.py
@@ -10,6 +10,8 @@
 MESH = pl.DeviceIdType.MESH
 CHUNK = 128
 SHARES = (2, 0, 2)
+PAIR = 2
+SLOTS = 5
 
 
 def turned(rows, by):
@@ -78,22 +80,37 @@
     for c in range(f_chunks + h_chunks):
         load(c).start()
 
+    lane, row, last = lax.rem(me, PAIR), me // PAIR, count // PAIR - 1
+    partner = me + 1 - PAIR * lane
+    around = (
+        (row >= 0, partner, (0, 1, 2)),
+        (row < last, me + PAIR, (0, 1)),
+        (row < last, partner + PAIR, (0, 1)),
+        (row > 0, me - PAIR, (0, 1, 2)),
+        (row > 0, partner - PAIR, (0, 1, 2)),
+    )
     barrier = pltpu.get_barrier_semaphore()
-
-    @pl.loop(1, count)
-    def _(d):
-        peer = lax.rem(me + d, count)
-        pl.semaphore_signal(barrier, inc=1, device_id={"tm": peer}, device_id_type=MESH)
-
-    pl.semaphore_wait(barrier, count - 1)
+    for there, peer, _ in around:
+
+        @pl.when(there)
+        def _():
+            pl.semaphore_signal(barrier, inc=1, device_id={"tm": peer}, device_id_type=MESH)
+
+    pl.semaphore_wait(barrier, 1 + PAIR * (lax.min(row, 1) + lax.min(last - row, 1)))
 
     pairs = ((z_ref, z_all), (m_ref, m_all), (g_ref, g_all))
 
-    def send(i, d):
-        peer = lax.rem(me + d, count)
+    def send(i, slot, peer):
         return pltpu.make_async_remote_copy(
             src_ref=pairs[i][0], dst_ref=pairs[i][1].at[me],
-            send_sem=send_sem.at[i, d], recv_sem=recv_sem.at[i, me],
+            send_sem=send_sem.at[i, slot], recv_sem=recv_sem.at[i, me],
+            device_id={"tm": peer}, device_id_type=MESH,
+        )
+
+    def relay(i, t, peer):
+        return pltpu.make_async_remote_copy(
+            src_ref=pairs[i][1].at[t], dst_ref=pairs[i][1].at[t],
+            send_sem=send_sem.at[i, SLOTS + t], recv_sem=recv_sem.at[i, t],
             device_id={"tm": peer}, device_id_type=MESH,
         )
 
@@ -101,13 +118,36 @@
         return pltpu.make_async_remote_copy(
             src_ref=pairs[i][0], dst_ref=pairs[i][1].at[t],
             send_sem=send_sem.at[i, 0], recv_sem=recv_sem.at[i, t],
-            device_id={"tm": lax.rem(me + 1, count)}, device_id_type=MESH,
+            device_id={"tm": partner}, device_id_type=MESH,
         )
 
-    @pl.loop(1, count)
-    def _(d):
-        for i in range(3):
-            send(i, d).start()
+    for slot, (there, peer, items) in enumerate(around):
+
+        @pl.when(there)
+        def _():
+            for i in items:
+                send(i, slot, peer).start()
+
+    def take_lower(onward):
+        @pl.loop(1, row + 1)
+        def _(d):
+            for side in range(PAIR):
+                t = PAIR * (row - d) + side
+                for i in (0, 1):
+                    arrival(i, t).wait_recv()
+                    if onward:
+                        relay(i, t, me + PAIR).start()
+
+    def take_upper(d):
+        for side in range(PAIR):
+            t = PAIR * (row + d) + side
+            for i in range(3):
+                arrival(i, t).wait_recv()
+
+            @pl.when(row > 0)
+            def _():
+                for i in range(3):
+                    relay(i, t, me - PAIR).start()
 
     z_all[me] = z_ref[...]
     m_all[me] = m_ref[...]
@@ -124,6 +164,11 @@
         if c * CHUNK >= q_plain:
             to = pl.ds(c * CHUNK - q_plain, CHUNK)
             ht_hi[:, to], ht_lo[:, to] = halves(h_in[rows, :].T)
+
+    @pl.when(row < last)
+    def _():
+        take_lower(True)
+
     for c in range(f_chunks):
         load(h_chunks + c).wait()
         if c * CHUNK >= f_plain:
@@ -136,10 +181,9 @@
     spread = (ht_in, *((h_hi, h_lo) if u_part else nothing))
 
     def block_of_steps(t, predicted):
-        @pl.when(t != me)
-        def _():
-            arrival(0, t).wait_recv()
-            arrival(1, t).wait_recv()
+        @pl.when((lax.rem(t, PAIR) == 1) & (row + (t + 1) // PAIR <= last))
+        def _():
+            take_upper((t + 1) // PAIR)
 
         weights = m_all[t].astype(jnp.float32) * mw_ref[...]
         readings = z_all[t]
@@ -153,15 +197,18 @@
             ps[t, k : k + 1, :] = predicted[:1]
         return predicted
 
-    lax.fori_loop(0, count, block_of_steps, apply(jnp.broadcast_to(x0_ref[...], (8, width)), *propagate))
+    first = apply(jnp.broadcast_to(x0_ref[...], (8, width)), *propagate)
+
+    @pl.when(row == last)
+    def _():
+        take_lower(False)
+
+    for i in range(3):
+        arrival(i, partner).wait_recv()
+
+    lax.fori_loop(0, count, block_of_steps, first)
 
     columns = pl.ds(pl.multiple_of(lax.axis_index("rows") * own, own), own)
-
-    @pl.loop(0, count)
-    def _(t):
-        @pl.when(t != me)
-        def _():
-            arrival(2, t).wait_recv()
 
     def smooth(lap, later):
         t = count - 1 - lap
@@ -183,10 +230,26 @@
 
     lax.fori_loop(0, count - me, smooth, ps[count - 1, steps - 1 : steps, columns])
 
-    @pl.loop(1, count)
-    def _(d):
-        for i in range(3):
-            send(i, d).wait_send()
+    for slot, (there, peer, items) in enumerate(around):
+
+        @pl.when(there)
+        def _():
+            for i in items:
+                send(i, slot, peer).wait_send()
+
+    @pl.when(row < last)
+    def _():
+        @pl.loop(0, PAIR * row)
+        def _(t):
+            for i in (0, 1):
+                relay(i, t, me + PAIR).wait_send()
+
+    @pl.when(row > 0)
+    def _():
+        @pl.loop(PAIR * (row + 1), count)
+        def _(t):
+            for i in range(3):
+                relay(i, t, me - PAIR).wait_send()
 
 
 def shares(width, measures):
@@ -228,7 +291,7 @@
             pltpu.VMEM((width - u_part, measures), jnp.float32),
             pltpu.VMEM((count, steps, width), jnp.float32),
             pltpu.VMEM((count, steps, width), jnp.float32),
-            pltpu.SemaphoreType.DMA((3, count)),
+            pltpu.SemaphoreType.DMA((3, SLOTS + count)),
             pltpu.SemaphoreType.DMA((3, count)),
             pltpu.SemaphoreType.DMA(((width + measures) // CHUNK,)),
         ],

time: 32.6 us -> 34.3 us (1.052)
  the two profiles are of different devices: /device:TPU:0 before, /device:TPU:30 now
where the time goes in v1:
time: 34.3 us; the launch traced here: 34 us
  Pallas kernels  33.4 us (97%)
  between operations  0.64 us (2%)
    pallas_call x1, Pallas kernels, body(): pl.pallas_call(kernel, out_shape=jax.ShapeDtypeStruct((2, steps, own), jn...  32.1 us
    pallas_call x1, Pallas kernels, body(): pl.pallas_call(parted, out_shape=(out, out), in_specs=[vmem], out_specs=(...  1.3 us

profile of v1, /device:TPU:30, one launch (start us, length us, event | category | flops | bytes accessed | tf_op | source)
XLA Modules:
  0.0 34.0 jit_solution(5841608752190531526)
XLA Ops:
  0.6 32.1 %shard_map.86.both_ref = f32[2,4,256]{2,1,0:T(4,128)} custom-call(f32[4,512]{1,0:T(4,128)} %z_ref.1, s32[4,512]{1,0:T(4,128)} %m_ref.1, f32[1024,1024]{1,0:T(8,128)} %f_hbm.1, f32[512,1024]{1,0:T(8,128)} %h_hbm.1, f32[1,512]{1,0:T(1,128)} %bitcast.3, f32[4,256]{1,0:T(4,128)} %g_ref.1, f32[1,1024]{1,0:T(1,128)} %bitcast.2), custom_call_target="tpu_custom_call" | custom-call | tf_op jit(solution)/shard_map/pallas_call | solution.py:274
  32.7 1.3 %shard_map.87 = (f32[4,256]{1,0:T(4,128)}, f32[4,256]{1,0:T(4,128)}) custom-call(f32[2,4,256]{2,1,0:T(4,128)} %shard_map.86.both_ref), custom_call_target="tpu_custom_call" | custom-call | tf_op jit(solution)/shard_map/pallas_call | solution.py:302

commit v2 on v0

--- a/solution.py
+++ b/solution.py
@@ -55,10 +55,10 @@
 
 
 def kernel(
-    z_ref, m_ref, f_hbm, h_hbm, mw_ref, g_ref, x0_ref,
+    z_ref, m_ref, f_hbm, h_hbm, mw_hbm, g_ref, x0_hbm,
     out_ref,
-    z_all, m_all, g_all, f_in, h_in, ft_hi, ft_lo, ht_hi, ht_lo, h_hi, h_lo, ht_in, xs, ps,
-    send_sem, recv_sem, load_sem,
+    mw_ref, x0_ref, z_all, m_all, g_all, f_in, h_in, ft_hi, ft_lo, ht_hi, ht_lo, h_hi, h_lo, ht_in, xs, ps,
+    send_sem, recv_sem, load_sem, own_sem,
 ):
     me = lax.axis_index("tm")
     count = lax.axis_size("tm")
@@ -75,9 +75,6 @@
         rows = pl.ds((c - h_chunks) * CHUNK, CHUNK)
         return pltpu.make_async_copy(f_hbm.at[rows], f_in.at[rows], load_sem.at[c])
 
-    for c in range(f_chunks + h_chunks):
-        load(c).start()
-
     barrier = pltpu.get_barrier_semaphore()
 
     @pl.loop(1, count)
@@ -85,9 +82,14 @@
         peer = lax.rem(me + d, count)
         pl.semaphore_signal(barrier, inc=1, device_id={"tm": peer}, device_id_type=MESH)
 
+    pairs = ((z_ref, z_all), (m_ref, m_all), (g_ref, g_all))
+    loads = [(source, target.at[me]) for source, target in pairs] + [(mw_hbm, mw_ref), (x0_hbm, x0_ref)]
+    own_loads = [pltpu.make_async_copy(*ends, own_sem.at[n]) for n, ends in enumerate(loads)]
+    for c in range(f_chunks + h_chunks):
+        load(c).start()
+    for copy in own_loads:
+        copy.start()
     pl.semaphore_wait(barrier, count - 1)
-
-    pairs = ((z_ref, z_all), (m_ref, m_all), (g_ref, g_all))
 
     def send(i, d):
         peer = lax.rem(me + d, count)
@@ -109,9 +111,8 @@
         for i in range(3):
             send(i, d).start()
 
-    z_all[me] = z_ref[...]
-    m_all[me] = m_ref[...]
-    g_all[me] = g_ref[...]
+    for copy in own_loads:
+        copy.wait()
 
     f_part, q_part, u_part = shares(width, measures)
     f_plain, q_plain, u_plain = width - f_part, measures - q_part, width - u_part
@@ -204,16 +205,18 @@
     width = f.shape[0]
     own = gain.shape[1]
     vmem = pl.BlockSpec(memory_space=pltpu.VMEM)
-    hbm = pl.BlockSpec(memory_space=pl.ANY)
+    hbm = pl.BlockSpec(memory_space=pltpu.HBM)
     out = jax.ShapeDtypeStruct((steps, own), jnp.float32)
     half = jnp.bfloat16
     f_part, q_part, u_part = shares(width, measures)
     both = pl.pallas_call(
         kernel,
         out_shape=jax.ShapeDtypeStruct((2, steps, own), jnp.float32),
-        in_specs=[vmem, vmem, hbm, hbm, vmem, vmem, vmem],
+        in_specs=[hbm] * 7,
         out_specs=vmem,
         scratch_shapes=[
+            pltpu.VMEM((1, measures), jnp.float32),
+            pltpu.VMEM((1, width), jnp.float32),
             pltpu.VMEM((count, steps, measures), jnp.float32),
             pltpu.VMEM((count, steps, measures), jnp.int32),
             pltpu.VMEM((count, steps, own), jnp.float32),
@@ -231,6 +234,7 @@
             pltpu.SemaphoreType.DMA((3, count)),
             pltpu.SemaphoreType.DMA((3, count)),
             pltpu.SemaphoreType.DMA(((width + measures) // CHUNK,)),
+            pltpu.SemaphoreType.DMA((5,)),
         ],
         compiler_params=pltpu.CompilerParams(
             collective_id=0, has_side_effects=True, vmem_limit_bytes=60 * 2**20

time: 32.6 us -> 32 us (0.982)
  Pallas kernels: 31.5 us -> 30.8 us
    pallas_call x1, Pallas kernels: 30.2 us -> 29.5 us  [body(): pl.pallas_call(kernel, out_shape=jax.ShapeDtypeStruct((2, steps, own), jn...]
where the time goes in v2:
time: 32 us; the launch traced here: 31.4 us
  Pallas kernels  30.8 us (96%)
  between operations  0.64 us (2%)
    pallas_call x1, Pallas kernels, body(): pl.pallas_call(kernel, out_shape=jax.ShapeDtypeStruct((2, steps, own), jn...  29.5 us
    pallas_call x1, Pallas kernels, body(): pl.pallas_call(parted, out_shape=(out, out), in_specs=[vmem], out_specs=(...  1.3 us

profile of v2, /device:TPU:0, one launch (start us, length us, event | category | flops | bytes accessed | tf_op | source)
XLA Modules:
  0.0 31.4 jit_solution(11745778167917746451)
XLA Ops:
  0.6 29.5 %shard_map.86.both_ref = f32[2,4,256]{2,1,0:T(4,128)} custom-call(f32[4,512]{1,0:T(4,128)} %z_ref.1, s32[4,512]{1,0:T(4,128)} %m_ref.1, f32[1024,1024]{1,0:T(8,128)} %f_hbm.1, f32[512,1024]{1,0:T(8,128)} %h_hbm.1, f32[1,512]{1,0:T(1,128)} %bitcast.3, f32[4,256]{1,0:T(4,128)} %g_ref.1, f32[1,1024]{1,0:T(1,128)} %bitcast.2), custom_call_target="tpu_custom_call" | custom-call | tf_op jit(solution)/shard_map/pallas_call | solution.py:212
  30.1 1.3 %shard_map.87 = (f32[4,256]{1,0:T(4,128)}, f32[4,256]{1,0:T(4,128)}) custom-call(f32[2,4,256]{2,1,0:T(4,128)} %shard_map.86.both_ref), custom_call_target="tpu_custom_call" | custom-call | tf_op jit(solution)/shard_map/pallas_call | solution.py:243

commit v3 on v2

--- a/solution.py
+++ b/solution.py
@@ -9,7 +9,9 @@
 
 MESH = pl.DeviceIdType.MESH
 CHUNK = 128
-SHARES = (2, 0, 2)
+BAND = 256
+PUSH_AT = 3
+SHARES = (4, 2)
 
 
 def turned(rows, by):
@@ -22,14 +24,14 @@
     return jnp.where(even, high, rows - high).astype(jnp.bfloat16)
 
 
-def apply(rows, plain, high, low):
-    outputs, depth = plain.shape
+def apply(rows, plain, firsts, high, low):
+    depth = plain.shape[1]
     if high is not None:
         left = split_rows(rows)
         upper = jnp.dot(left, high[...], preferred_element_type=jnp.float32)
         lower = jnp.dot(left, low[...], preferred_element_type=jnp.float32)
     parts = []
-    for first in range(0, outputs, CHUNK):
+    for first in firsts:
         sums = None
         for at in range(0, depth, CHUNK):
             block = plain[first : first + CHUNK, at : at + CHUNK].reshape(CHUNK // 8, 8, CHUNK)
@@ -39,10 +41,10 @@
         for by in (4, 2, 1):
             part += turned(part, by)
         parts.append(part)
-    if high is not None:
-        total = upper + lower
-        parts.append(total + turned(total, 1))
-    return jnp.concatenate(parts, axis=1)
+    if high is None:
+        return parts, []
+    total = upper + lower
+    return parts, [total + turned(total, 1)]
 
 
 def matrix_part(size, eighths):
@@ -57,7 +59,7 @@
 def kernel(
     z_ref, m_ref, f_hbm, h_hbm, mw_hbm, g_ref, x0_hbm,
     out_ref,
-    mw_ref, x0_ref, z_all, m_all, g_all, f_in, h_in, ft_hi, ft_lo, ht_hi, ht_lo, h_hi, h_lo, ht_in, xs, ps,
+    mw_ref, x0_ref, z_all, m_all, g_all, gf, h_in, band_hi, band_lo, ft_hi, ft_lo, h_hi, h_lo, ht_in, xs, ps,
     send_sem, recv_sem, load_sem, own_sem,
 ):
     me = lax.axis_index("tm")
@@ -73,7 +75,8 @@
             rows = pl.ds(c * CHUNK, CHUNK)
             return pltpu.make_async_copy(h_hbm.at[rows], h_in.at[rows], load_sem.at[c])
         rows = pl.ds((c - h_chunks) * CHUNK, CHUNK)
-        return pltpu.make_async_copy(f_hbm.at[rows], f_in.at[rows], load_sem.at[c])
+        target = gf.at[pl.ds(measures + (c - h_chunks) * CHUNK, CHUNK)]
+        return pltpu.make_async_copy(f_hbm.at[rows], target, load_sem.at[c])
 
     barrier = pltpu.get_barrier_semaphore()
 
@@ -89,13 +92,13 @@
         load(c).start()
     for copy in own_loads:
         copy.start()
-    pl.semaphore_wait(barrier, count - 1)
-
-    def send(i, d):
-        peer = lax.rem(me + d, count)
+    for copy in own_loads:
+        copy.wait()
+
+    def send(i, peer):
         return pltpu.make_async_remote_copy(
             src_ref=pairs[i][0], dst_ref=pairs[i][1].at[me],
-            send_sem=send_sem.at[i, d], recv_sem=recv_sem.at[i, me],
+            send_sem=send_sem.at[i, peer], recv_sem=recv_sem.at[i, me],
             device_id={"tm": peer}, device_id_type=MESH,
         )
 
@@ -106,37 +109,58 @@
             device_id={"tm": lax.rem(me + 1, count)}, device_id_type=MESH,
         )
 
-    @pl.loop(1, count)
-    def _(d):
-        for i in range(3):
-            send(i, d).start()
-
-    for copy in own_loads:
-        copy.wait()
-
-    f_part, q_part, u_part = shares(width, measures)
-    f_plain, q_plain, u_plain = width - f_part, measures - q_part, width - u_part
+    def push():
+        pl.semaphore_wait(barrier, count - 1)
+
+        @pl.loop(1, count)
+        def _(d):
+            peer = lax.rem(me + count - d, count)
+            for i in (0, 1):
+                send(i, peer).start()
+
+        @pl.loop(0, me)
+        def _(peer):
+            send(2, peer).start()
+
+    f_part, u_part = shares(width)
+    u_plain = width - u_part
+    bands = width // BAND
     for c in range(h_chunks):
         load(c).wait()
         rows = pl.ds(c * CHUNK, CHUNK)
         ht_in[:, rows] = h_in[rows, :u_plain].T
         if u_part:
             h_hi[rows, :], h_lo[rows, :] = halves(h_in[rows, u_plain:])
-        if c * CHUNK >= q_plain:
-            to = pl.ds(c * CHUNK - q_plain, CHUNK)
-            ht_hi[:, to], ht_lo[:, to] = halves(h_in[rows, :].T)
-    for c in range(f_chunks):
-        load(h_chunks + c).wait()
-        if c * CHUNK >= f_plain:
-            to = pl.ds(c * CHUNK - f_plain, CHUNK)
-            ft_hi[:, to], ft_lo[:, to] = halves(f_in[pl.ds(c * CHUNK, CHUNK), :].T)
-
-    nothing = (None, None)
-    propagate = (f_in.at[:f_plain], *((ft_hi, ft_lo) if f_part else nothing))
-    observe = (h_in.at[:q_plain], *((ht_hi, ht_lo) if q_part else nothing))
-    spread = (ht_in, *((h_hi, h_lo) if u_part else nothing))
-
-    def block_of_steps(t, predicted):
+        for b in range(bands):
+            band_hi[b, rows, :], band_lo[b, rows, :] = halves(h_in[rows, b * BAND : (b + 1) * BAND])
+    for b in range(bands):
+        if b == PUSH_AT:
+            push()
+        for c in range(b * BAND // CHUNK, (b + 1) * BAND // CHUNK):
+            load(h_chunks + c).wait()
+        high, low = halves(gf[measures + b * BAND : measures + (b + 1) * BAND, :])
+        product = functools.partial(jnp.dot, preferred_element_type=jnp.float32)
+        term = product(band_hi[b], high) + product(band_lo[b], high) + product(band_hi[b], low)
+        gf[:measures, :] = term if b == 0 else gf[:measures, :] + term
+        for first in range(b * BAND, min((b + 1) * BAND, f_part), CHUNK):
+            to = pl.ds(first, CHUNK)
+            ft_hi[:, to], ft_lo[:, to] = halves(gf[measures + first : measures + first + CHUNK, :].T)
+
+    def advance(state):
+        firsts = [*range(0, measures, CHUNK), *range(measures + f_part, measures + width, CHUNK)]
+        parts, shared = apply(state, gf, firsts, *((ft_hi, ft_lo) if f_part else (None, None)))
+        seen = jnp.concatenate(parts[: measures // CHUNK], axis=1)
+        return jnp.concatenate([*shared, *parts[measures // CHUNK :]], axis=1), seen
+
+    def spread(change):
+        parts, shared = apply(
+            change, ht_in, range(0, u_plain, CHUNK), *((h_hi, h_lo) if u_part else (None, None))
+        )
+        return jnp.concatenate([*parts, *shared], axis=1)
+
+    def block_of_steps(t, carried):
+        predicted, seen = carried
+
         @pl.when(t != me)
         def _():
             arrival(0, t).wait_recv()
@@ -146,23 +170,20 @@
         readings = z_all[t]
         alike = functools.partial(jnp.broadcast_to, shape=(8, measures))
         for k in range(steps):
-            seen = apply(predicted, *observe)
             change = alike(weights[k : k + 1]) * (alike(readings[k : k + 1]) - seen)
-            state = predicted + apply(change, *spread)
-            predicted = apply(state, *propagate)
+            state = predicted + spread(change)
+            predicted, seen = advance(state)
             xs[t, k : k + 1, :] = state[:1]
             ps[t, k : k + 1, :] = predicted[:1]
-        return predicted
-
-    lax.fori_loop(0, count, block_of_steps, apply(jnp.broadcast_to(x0_ref[...], (8, width)), *propagate))
+        return predicted, seen
+
+    lax.fori_loop(0, count, block_of_steps, advance(jnp.broadcast_to(x0_ref[...], (8, width))))
 
     columns = pl.ds(pl.multiple_of(lax.axis_index("rows") * own, own), own)
 
-    @pl.loop(0, count)
+    @pl.loop(me + 1, count)
     def _(t):
-        @pl.when(t != me)
-        def _():
-            arrival(2, t).wait_recv()
+        arrival(2, t).wait_recv()
 
     def smooth(lap, later):
         t = count - 1 - lap
@@ -186,12 +207,16 @@
 
     @pl.loop(1, count)
     def _(d):
-        for i in range(3):
-            send(i, d).wait_send()
-
-
-def shares(width, measures):
-    return tuple(map(matrix_part, (width, measures, width), SHARES))
+        for i in (0, 1):
+            send(i, lax.rem(me + count - d, count)).wait_send()
+
+    @pl.loop(0, me)
+    def _(peer):
+        send(2, peer).wait_send()
+
+
+def shares(width):
+    return tuple(matrix_part(width, eighths) for eighths in SHARES)
 
 
 def parted(both_ref, mean_ref, rec_ref):
@@ -208,7 +233,7 @@
     hbm = pl.BlockSpec(memory_space=pltpu.HBM)
     out = jax.ShapeDtypeStruct((steps, own), jnp.float32)
     half = jnp.bfloat16
-    f_part, q_part, u_part = shares(width, measures)
+    f_part, u_part = shares(width)
     both = pl.pallas_call(
         kernel,
         out_shape=jax.ShapeDtypeStruct((2, steps, own), jnp.float32),
@@ -220,12 +245,12 @@
             pltpu.VMEM((count, steps, measures), jnp.float32),
             pltpu.VMEM((count, steps, measures), jnp.int32),
             pltpu.VMEM((count, steps, own), jnp.float32),
-            pltpu.VMEM((width, width), jnp.float32),
+            pltpu.VMEM((measures + width, width), jnp.float32),
             pltpu.VMEM((measures, width), jnp.float32),
+            pltpu.VMEM((width // BAND, measures, BAND), half),
+            pltpu.VMEM((width // BAND, measures, BAND), half),
             pltpu.VMEM((width, max(f_part, CHUNK)), half),
             pltpu.VMEM((width, max(f_part, CHUNK)), half),
-            pltpu.VMEM((width, max(q_part, CHUNK)), half),
-            pltpu.VMEM((width, max(q_part, CHUNK)), half),
             pltpu.VMEM((measures, max(u_part, CHUNK)), half),
             pltpu.VMEM((measures, max(u_part, CHUNK)), half),
             pltpu.VMEM((width - u_part, measures), jnp.float32),

time: 32 us -> 29.7 us (0.928)
  the two profiles are of different devices: /device:TPU:0 before, /device:TPU:12 now
where the time goes in v3:
time: 29.7 us; the launch traced here: 29.4 us
  Pallas kernels  28.8 us (97%)
  between operations  0.64 us (2%)
    pallas_call x1, Pallas kernels, body(): pl.pallas_call(kernel, out_shape=jax.ShapeDtypeStruct((2, steps, own), jn...  27.5 us
    pallas_call x1, Pallas kernels, body(): pl.pallas_call(parted, out_shape=(out, out), in_specs=[vmem], out_specs=(...  1.3 us

profile of v3, /device:TPU:12, one launch (start us, length us, event | category | flops | bytes accessed | tf_op | source)
XLA Modules:
  0.0 29.4 jit_solution(4614030614319147578)
XLA Ops:
  0.6 27.5 %shard_map.86.both_ref = f32[2,4,256]{2,1,0:T(4,128)} custom-call(f32[4,512]{1,0:T(4,128)} %z_ref.1, s32[4,512]{1,0:T(4,128)} %m_ref.1, f32[1024,1024]{1,0:T(8,128)} %f_hbm.1, f32[512,1024]{1,0:T(8,128)} %h_hbm.1, f32[1,512]{1,0:T(1,128)} %bitcast.3, f32[4,256]{1,0:T(4,128)} %g_ref.1, f32[1,1024]{1,0:T(1,128)} %bitcast.2), custom_call_target="tpu_custom_call" | custom-call | tf_op jit(solution)/shard_map/pallas_call | solution.py:237
  28.1 1.3 %shard_map.87 = (f32[4,256]{1,0:T(4,128)}, f32[4,256]{1,0:T(4,128)}) custom-call(f32[2,4,256]{2,1,0:T(4,128)} %shard_map.86.both_ref), custom_call_target="tpu_custom_call" | custom-call | tf_op jit(solution)/shard_map/pallas_call | solution.py:268

commit v4 on v3

--- a/solution.py
+++ b/solution.py
@@ -10,7 +10,7 @@
 MESH = pl.DeviceIdType.MESH
 CHUNK = 128
 BAND = 256
-PUSH_AT = 3
+PUSH_AT = 2
 SHARES = (4, 2)
 
 
@@ -59,7 +59,7 @@
 def kernel(
     z_ref, m_ref, f_hbm, h_hbm, mw_hbm, g_ref, x0_hbm,
     out_ref,
-    mw_ref, x0_ref, z_all, m_all, g_all, gf, h_in, band_hi, band_lo, ft_hi, ft_lo, h_hi, h_lo, ht_in, xs, ps,
+    mw_ref, x0_ref, z_all, m_all, g_all, gf, h_in, ft_hi, ft_lo, h_hi, h_lo, ht_in, xs, ps,
     send_sem, recv_sem, load_sem, own_sem,
 ):
     me = lax.axis_index("tm")
@@ -127,24 +127,30 @@
     bands = width // BAND
     for c in range(h_chunks):
         load(c).wait()
-        rows = pl.ds(c * CHUNK, CHUNK)
-        ht_in[:, rows] = h_in[rows, :u_plain].T
-        if u_part:
-            h_hi[rows, :], h_lo[rows, :] = halves(h_in[rows, u_plain:])
-        for b in range(bands):
-            band_hi[b, rows, :], band_lo[b, rows, :] = halves(h_in[rows, b * BAND : (b + 1) * BAND])
     for b in range(bands):
         if b == PUSH_AT:
             push()
-        for c in range(b * BAND // CHUNK, (b + 1) * BAND // CHUNK):
-            load(h_chunks + c).wait()
+        if b <= PUSH_AT:
+            for c in range(b * BAND // CHUNK, ((b + 1) if b < PUSH_AT else bands) * BAND // CHUNK):
+                load(h_chunks + c).wait()
         high, low = halves(gf[measures + b * BAND : measures + (b + 1) * BAND, :])
+        h_high, h_low = halves(h_in[:, b * BAND : (b + 1) * BAND])
         product = functools.partial(jnp.dot, preferred_element_type=jnp.float32)
-        term = product(band_hi[b], high) + product(band_lo[b], high) + product(band_hi[b], low)
+        term = product(h_high, high) + product(h_low, high) + product(h_high, low)
         gf[:measures, :] = term if b == 0 else gf[:measures, :] + term
+        if b == 0:
+            ht_in[...] = h_in[:, :u_plain].T
+            if u_part:
+                h_hi[...], h_lo[...] = halves(h_in[:, u_plain:])
         for first in range(b * BAND, min((b + 1) * BAND, f_part), CHUNK):
             to = pl.ds(first, CHUNK)
             ft_hi[:, to], ft_lo[:, to] = halves(gf[measures + first : measures + first + CHUNK, :].T)
+
+    def start(state):
+        parts, _ = apply(state, gf, range(measures, measures + width, CHUNK), None, None)
+        predicted = jnp.concatenate(parts, axis=1)
+        parts, _ = apply(predicted, h_in, range(0, measures, CHUNK), None, None)
+        return predicted, jnp.concatenate(parts, axis=1)
 
     def advance(state):
         firsts = [*range(0, measures, CHUNK), *range(measures + f_part, measures + width, CHUNK)]
@@ -177,7 +183,7 @@
             ps[t, k : k + 1, :] = predicted[:1]
         return predicted, seen
 
-    lax.fori_loop(0, count, block_of_steps, advance(jnp.broadcast_to(x0_ref[...], (8, width))))
+    lax.fori_loop(0, count, block_of_steps, start(jnp.broadcast_to(x0_ref[...], (8, width))))
 
     columns = pl.ds(pl.multiple_of(lax.axis_index("rows") * own, own), own)
 
@@ -247,8 +253,6 @@
             pltpu.VMEM((count, steps, own), jnp.float32),
             pltpu.VMEM((measures + width, width), jnp.float32),
             pltpu.VMEM((measures, width), jnp.float32),
-            pltpu.VMEM((width // BAND, measures, BAND), half),
-            pltpu.VMEM((width // BAND, measures, BAND), half),
             pltpu.VMEM((width, max(f_part, CHUNK)), half),
             pltpu.VMEM((width, max(f_part, CHUNK)), half),
             pltpu.VMEM((measures, max(u_part, CHUNK)), half),

time: 29.7 us -> 28.1 us (0.946)
  the two profiles are of different devices: /device:TPU:12 before, /device:TPU:0 now
where the time goes in v4:
time: 28.1 us; the launch traced here: 27.8 us
  Pallas kernels  27.2 us (97%)
  between operations  0.64 us (2%)
    pallas_call x1, Pallas kernels, body(): pl.pallas_call(kernel, out_shape=jax.ShapeDtypeStruct((2, steps, own), jn...  25.9 us
    pallas_call x1, Pallas kernels, body(): pl.pallas_call(parted, out_shape=(out, out), in_specs=[vmem], out_specs=(...  1.3 us

profile of v4, /device:TPU:0, one launch (start us, length us, event | category | flops | bytes accessed | tf_op | source)
XLA Modules:
  0.0 27.8 jit_solution(17313378963806591368)
XLA Ops:
  0.6 25.9 %shard_map.86.both_ref = f32[2,4,256]{2,1,0:T(4,128)} custom-call(f32[4,512]{1,0:T(4,128)} %z_ref.1, s32[4,512]{1,0:T(4,128)} %m_ref.1, f32[1024,1024]{1,0:T(8,128)} %f_hbm.1, f32[512,1024]{1,0:T(8,128)} %h_hbm.1, f32[1,512]{1,0:T(1,128)} %bitcast.3, f32[4,256]{1,0:T(4,128)} %g_ref.1, f32[1,1024]{1,0:T(1,128)} %bitcast.2), custom_call_target="tpu_custom_call" | custom-call | tf_op jit(solution)/shard_map/pallas_call | solution.py:243
  26.5 1.3 %shard_map.87 = (f32[4,256]{1,0:T(4,128)}, f32[4,256]{1,0:T(4,128)}) custom-call(f32[2,4,256]{2,1,0:T(4,128)} %shard_map.86.both_ref), custom_call_target="tpu_custom_call" | custom-call | tf_op jit(solution)/shard_map/pallas_call | solution.py:272

commit v5 on v4

--- a/solution.py
+++ b/solution.py
@@ -11,7 +11,7 @@
 CHUNK = 128
 BAND = 256
 PUSH_AT = 2
-SHARES = (4, 2)
+SHARES = (4, 1)
 
 
 def turned(rows, by):
@@ -88,7 +88,8 @@
     pairs = ((z_ref, z_all), (m_ref, m_all), (g_ref, g_all))
     loads = [(source, target.at[me]) for source, target in pairs] + [(mw_hbm, mw_ref), (x0_hbm, x0_ref)]
     own_loads = [pltpu.make_async_copy(*ends, own_sem.at[n]) for n, ends in enumerate(loads)]
-    for c in range(f_chunks + h_chunks):
+    early = h_chunks + BAND // CHUNK
+    for c in range(early):
         load(c).start()
     for copy in own_loads:
         copy.start()
@@ -114,7 +115,7 @@
 
         @pl.loop(1, count)
         def _(d):
-            peer = lax.rem(me + count - d, count)
+            peer = lax.rem(me + d, count)
             for i in (0, 1):
                 send(i, peer).start()
 
@@ -133,10 +134,15 @@
         if b <= PUSH_AT:
             for c in range(b * BAND // CHUNK, ((b + 1) if b < PUSH_AT else bands) * BAND // CHUNK):
                 load(h_chunks + c).wait()
+        if b == 0:
+            for c in range(early, f_chunks + h_chunks):
+                load(c).start()
         high, low = halves(gf[measures + b * BAND : measures + (b + 1) * BAND, :])
         h_high, h_low = halves(h_in[:, b * BAND : (b + 1) * BAND])
         product = functools.partial(jnp.dot, preferred_element_type=jnp.float32)
-        term = product(h_high, high) + product(h_low, high) + product(h_high, low)
+        term = product(
+            jnp.concatenate([h_high, h_low, h_high], axis=1), jnp.concatenate([high, high, low], axis=0)
+        )
         gf[:measures, :] = term if b == 0 else gf[:measures, :] + term
         if b == 0:
             ht_in[...] = h_in[:, :u_plain].T
@@ -214,7 +220,7 @@
     @pl.loop(1, count)
     def _(d):
         for i in (0, 1):
-            send(i, lax.rem(me + count - d, count)).wait_send()
+            send(i, lax.rem(me + d, count)).wait_send()
 
     @pl.loop(0, me)
     def _(peer):

time: 28.1 us -> 27.9 us (level)
  no operation moved by 1% of the time
where the time goes in v5:
time: 27.9 us; the launch traced here: 27.6 us
  Pallas kernels  27 us (97%)
  between operations  0.64 us (2%)
    pallas_call x1, Pallas kernels, body(): pl.pallas_call(kernel, out_shape=jax.ShapeDtypeStruct((2, steps, own), jn...  25.7 us
    pallas_call x1, Pallas kernels, body(): pl.pallas_call(parted, out_shape=(out, out), in_specs=[vmem], out_specs=(...  1.3 us

profile of v5, /device:TPU:0, one launch (start us, length us, event | category | flops | bytes accessed | tf_op | source)
XLA Modules:
  0.0 27.6 jit_solution(10428090339355148604)
XLA Ops:
  0.6 25.7 %shard_map.86.both_ref = f32[2,4,256]{2,1,0:T(4,128)} custom-call(f32[4,512]{1,0:T(4,128)} %z_ref.1, s32[4,512]{1,0:T(4,128)} %m_ref.1, f32[1024,1024]{1,0:T(8,128)} %f_hbm.1, f32[512,1024]{1,0:T(8,128)} %h_hbm.1, f32[1,512]{1,0:T(1,128)} %bitcast.3, f32[4,256]{1,0:T(4,128)} %g_ref.1, f32[1,1024]{1,0:T(1,128)} %bitcast.2), custom_call_target="tpu_custom_call" | custom-call | tf_op jit(solution)/shard_map/pallas_call | solution.py:249
  26.3 1.3 %shard_map.87 = (f32[4,256]{1,0:T(4,128)}, f32[4,256]{1,0:T(4,128)}) custom-call(f32[2,4,256]{2,1,0:T(4,128)} %shard_map.86.both_ref), custom_call_target="tpu_custom_call" | custom-call | tf_op jit(solution)/shard_map/pallas_call | solution.py:278

commit v6 on v5

--- a/solution.py
+++ b/solution.py
@@ -125,30 +125,30 @@
 
     f_part, u_part = shares(width)
     u_plain = width - u_part
-    bands = width // BAND
     for c in range(h_chunks):
         load(c).wait()
-    for b in range(bands):
+    edges = [*range(0, PUSH_AT * BAND + 1, BAND), width]
+    for b, (low_edge, high_edge) in enumerate(zip(edges, edges[1:])):
         if b == PUSH_AT:
             push()
-        if b <= PUSH_AT:
-            for c in range(b * BAND // CHUNK, ((b + 1) if b < PUSH_AT else bands) * BAND // CHUNK):
-                load(h_chunks + c).wait()
+        for c in range(low_edge // CHUNK, high_edge // CHUNK):
+            load(h_chunks + c).wait()
         if b == 0:
             for c in range(early, f_chunks + h_chunks):
                 load(c).start()
-        high, low = halves(gf[measures + b * BAND : measures + (b + 1) * BAND, :])
-        h_high, h_low = halves(h_in[:, b * BAND : (b + 1) * BAND])
-        product = functools.partial(jnp.dot, preferred_element_type=jnp.float32)
-        term = product(
-            jnp.concatenate([h_high, h_low, h_high], axis=1), jnp.concatenate([high, high, low], axis=0)
+        high, low = halves(gf[measures + low_edge : measures + high_edge, :])
+        h_high, h_low = halves(h_in[:, low_edge:high_edge])
+        term = jnp.dot(
+            jnp.concatenate([h_high, h_low, h_high], axis=1),
+            jnp.concatenate([high, high, low], axis=0),
+            preferred_element_type=jnp.float32,
         )
         gf[:measures, :] = term if b == 0 else gf[:measures, :] + term
         if b == 0:
             ht_in[...] = h_in[:, :u_plain].T
             if u_part:
                 h_hi[...], h_lo[...] = halves(h_in[:, u_plain:])
-        for first in range(b * BAND, min((b + 1) * BAND, f_part), CHUNK):
+        for first in range(low_edge, min(high_edge, f_part), CHUNK):
             to = pl.ds(first, CHUNK)
             ft_hi[:, to], ft_lo[:, to] = halves(gf[measures + first : measures + first + CHUNK, :].T)
 

time: 27.9 us -> 27.9 us (level)
  no operation moved by 1% of the time
where the time goes in v6:
time: 27.9 us; the launch traced here: 27.7 us
  Pallas kernels  27 us (97%)
  between operations  0.64 us (2%)
    pallas_call x1, Pallas kernels, body(): pl.pallas_call(kernel, out_shape=jax.ShapeDtypeStruct((2, steps, own), jn...  25.7 us
    pallas_call x1, Pallas kernels, body(): pl.pallas_call(parted, out_shape=(out, out), in_specs=[vmem], out_specs=(...  1.3 us

profile of v6, /device:TPU:0, one launch (start us, length us, event | category | flops | bytes accessed | tf_op | source)
XLA Modules:
  0.0 27.7 jit_solution(4936004408766606361)
XLA Ops:
  0.6 25.7 %shard_map.86.both_ref = f32[2,4,256]{2,1,0:T(4,128)} custom-call(f32[4,512]{1,0:T(4,128)} %z_ref.1, s32[4,512]{1,0:T(4,128)} %m_ref.1, f32[1024,1024]{1,0:T(8,128)} %f_hbm.1, f32[512,1024]{1,0:T(8,128)} %h_hbm.1, f32[1,512]{1,0:T(1,128)} %bitcast.3, f32[4,256]{1,0:T(4,128)} %g_ref.1, f32[1,1024]{1,0:T(1,128)} %bitcast.2), custom_call_target="tpu_custom_call" | custom-call | tf_op jit(solution)/shard_map/pallas_call | solution.py:249
  26.4 1.3 %shard_map.87 = (f32[4,256]{1,0:T(4,128)}, f32[4,256]{1,0:T(4,128)}) custom-call(f32[2,4,256]{2,1,0:T(4,128)} %shard_map.86.both_ref), custom_call_target="tpu_custom_call" | custom-call | tf_op jit(solution)/shard_map/pallas_call | solution.py:278
